TPU v7x, 32 devices: a whole 2x2x4 slice. The times are simulated.
32 devices in a mesh: row: 4 (over z), col: 8 (over y, x, core).
Axes of the slice: x: 2, y: 2, z: 4, core: 2. Of those that a mesh axis runs over, the one named last changes fastest.
Arguments:
- gaussian_sketch: bfloat16 [16384, 256], P(('col', 'row')), may hold values from -6 to 6
- block_values: bfloat16 [8192, 128, 128], P(('row', 'col')), may hold values from -6 to 6
- block_rows: int32 [8192], P(('row', 'col')), may hold values from 0 to 127, as said below
- block_columns: int32 [8192], P(('row', 'col')), may hold values from 0 to 127, as said below
Outputs:
- range_basis: float32 [16384, 256], P(('row', 'col'))
- upper_factor: float32 [256, 256], replicated
Inputs may be any that keep to these rules, and one draw needn't show every extreme that they name: `block_rows`: entry k * 256 + m, k = i * 8 + j, names a block row in [i * 32, (i + 1) * 32); no (row, column) pair is named twice. `block_columns`: entry k * 256 + m, k = i * 8 + j, names a block column in [j * 16, (j + 1) * 16).
All inputs are finite; a program needn't handle non-finite values.
Results may differ from a plain program's by a relative error of at most 0.0003.
Values may be sent and summed in bfloat16 or wider, within the bound.
No kernel may reach another device: no remote copies, remote signals or barrier semaphores. Data moves between devices by JAX's collectives and lax.ppermute only.
A program may use at most 128 MiB of HBM per device.

v0:
```python
import math
import jax
import jax.numpy as jnp
from jax import lax
from jax.sharding import PartitionSpec as P

PANEL = 128


def upper_parts(gram):
    lower_factor = jnp.linalg.cholesky(gram)
    identity = jnp.eye(gram.shape[0], dtype=gram.dtype)
    inverse = lax.linalg.triangular_solve(lower_factor, identity, left_side=True, lower=True)
    return (lower_factor.T, inverse.T)


def tile_product(sketch_blocks, block_values, local_rows, local_cols, tile_rows):
    group_size = math.gcd(block_values.shape[0], 64)
    col_width = sketch_blocks.shape[2]

    def advance(counter, summed):
        offset = (counter * group_size).astype(jnp.int32)
        values = lax.dynamic_slice_in_dim(block_values, offset, group_size, 0)
        row_ids = lax.dynamic_slice_in_dim(local_rows, offset, group_size, 0)
        col_ids = lax.dynamic_slice_in_dim(local_cols, offset, group_size, 0)
        picked = jnp.take(sketch_blocks, col_ids, axis=0)
        product = jnp.einsum("gab,gbs->gas", values, picked, preferred_element_type=jnp.float32)
        return summed.at[row_ids].add(product)

    initial = jnp.zeros((tile_rows, block_values.shape[1], col_width), jnp.float32)
    summed = lax.fori_loop(0, block_values.shape[0] // group_size, advance, initial)
    return summed.reshape(tile_rows * block_values.shape[1], col_width)


def on_device(gaussian_sketch, block_values, block_rows, block_columns):
    high = lax.Precision.HIGHEST
    size_row = lax.axis_size("row")
    size_col = lax.axis_size("col")
    shard_rows = gaussian_sketch.shape[0]
    block_size = block_values.shape[1]
    grid_rows = shard_rows * size_col // block_size
    grid_cols = shard_rows * size_row // block_size
    local_rows = block_rows - lax.axis_index("row") * grid_rows
    local_cols = block_columns - lax.axis_index("col") * grid_cols
    gathered = lax.all_gather(gaussian_sketch, "row", axis=0, tiled=True)
    sketch_blocks = gathered.reshape(grid_cols, block_size, gathered.shape[1])
    partial_value = tile_product(sketch_blocks, block_values, local_rows, local_cols, grid_rows)
    sketched = lax.psum_scatter(partial_value, "col", scatter_dimension=0, tiled=True)
    first_part = sketched[:, :PANEL]
    second_part = sketched[:, PANEL:]
    order_total = shard_rows * size_row * size_col
    gram_one = (
        lax.psum(jnp.dot(first_part.T, first_part, precision=high), ("row", "col")) / order_total
    )
    upper_one, inverse_one = upper_parts(gram_one)
    basis_one = jnp.dot(first_part, inverse_one, precision=high)
    coupling = (
        lax.psum(jnp.dot(basis_one.T, second_part, precision=high), ("row", "col")) / order_total
    )
    remainder = second_part - jnp.dot(basis_one, coupling, precision=high)
    gram_two = (
        lax.psum(jnp.dot(remainder.T, remainder, precision=high), ("row", "col")) / order_total
    )
    upper_two, inverse_two = upper_parts(gram_two)
    basis_two = jnp.dot(remainder, inverse_two, precision=high)
    range_basis = jnp.concatenate([basis_one, basis_two], axis=1)
    top_rows = jnp.concatenate([upper_one, coupling], axis=1)
    bottom_rows = jnp.concatenate([jnp.zeros_like(upper_two), upper_two], axis=1)
    upper_factor = jnp.concatenate([top_rows, bottom_rows], axis=0)
    return (range_basis, upper_factor)


def solution(mesh):
    return jax.shard_map(
        on_device,
        mesh=mesh,
        in_specs=(
            P(("col", "row"), None),
            P(("row", "col"), None, None),
            P(("row", "col")),
            P(("row", "col")),
        ),
        out_specs=(P(("row", "col"), None), P()),
        check_vma=False,
    )
```

profile of v0, /device:TPU:1, one launch (start us, length us, event | category | flops | bytes accessed | tf_op | source)
XLA Modules:
  0.0 643.8 jit_solution(3256187784970648376)
XLA Ops:
  7.2 0.0 all-gather.2.cloned.1.call-start
  7.2 0.7 all-gather.2.cloned.1.call-update
  7.9 0.0 reduce-scatter.2.cloned.1.call-start
  8.0 0.7 broadcast_subtract_fusion
  8.7 30.8 %all-gather.2.cloned.1.call-done = bf16[2048,256]{1,0:T(8,128)(2,1)} async-done(((bf16[512,256]{1,0:T(8,128)(2,1)}), bf16[2048,256]{1,0:T(8,128)(2,1)}) %all-gather.2.cloned.1.call-update) | async-done | bytes 1048592 | tf_op jit(solution)/shard_map/all_gather | solution.py:45
  39.5 2.5 broadcast_in_dim.36
  41.9 0.0 copy-done
  41.9 118.3 %while.13 = (s32[]{:T(128)}, f32[32,128,256]{2,1,0:T(8,128)}, s32[256]{0:T(256)S(1)}, bf16[256,128,128]{2,1,0:T(8,128)(2,1)}, s32[256]{0:T(256)S(1)}, /*index=5*...) while((s32[]{:T(128)}, f32[32,128,256]{2,1,0:T(8,128)}, s32[256]{0:T(256)S(1)}, ...), condition=%wide.region_2.3_spmd, body=%wide.region_0.2_spmd.sunk | while | flops 541066816 | bytes 48240672 | solution.py:31
  41.9 0.1 compare_and_fusion.2
  42.0 2.8 gather_fusion
  44.8 7.4 %fusion.38 = f32[64,128,256]{2,1,0:T(8,128)} fusion(bf16[64,128,256]{2,1,0:T(8,128)(2,1)} %gather_fusion, pred[64]{0:T(512)(128)(4,1)S(1)} %get-tuple-element.176, bf16[256,128,128]{2,1,0:T(8,128)(2,1)} %get-tuple-element.200, s32[]{:T(128)S(6)} %select_n.59), kind=kOutput, calls=%fused_computation.2.clone.1 | convolution fusion | flops 538968064 | bytes 14680132 | tf_op jit(solution)/shard_map/while/body/eval_jaxpr/gab,gbs->gas/dot_general | solution.py:27
  52.2 0.1 compare_select_fusion.4
  52.3 19.2 %scatter_fusion = f32[32,128,256]{2,1,0:T(8,128)} fusion(f32[32,128,256]{2,1,0:T(8,128)} %get-tuple-element.188, s32[64]{0:T(128)S(1)} %compare_select_fusion.4, f32[64,128,256]{2,1,0:T(8,128)} %fusion.38), kind=kCustom, calls=%fused_computation.1.clone.1 | custom fusion | flops 2097152 | bytes 25166080 | tf_op jit(solution)/shard_map/while/body/eval_jaxpr/scatter-add | solution.py:28
  71.4 0.1 compare_and_fusion.2
  71.5 2.8 gather_fusion
  74.3 7.4 %fusion.38 = f32[64,128,256]{2,1,0:T(8,128)} fusion(bf16[64,128,256]{2,1,0:T(8,128)(2,1)} %gather_fusion, pred[64]{0:T(512)(128)(4,1)S(1)} %get-tuple-element.176, bf16[256,128,128]{2,1,0:T(8,128)(2,1)} %get-tuple-element.200, s32[]{:T(128)S(6)} %select_n.59), kind=kOutput, calls=%fused_computation.2.clone.1 | convolution fusion | flops 538968064 | bytes 14680132 | tf_op jit(solution)/shard_map/while/body/eval_jaxpr/gab,gbs->gas/dot_general | solution.py:27
  81.7 0.1 compare_select_fusion.4
  81.7 19.1 %scatter_fusion = f32[32,128,256]{2,1,0:T(8,128)} fusion(f32[32,128,256]{2,1,0:T(8,128)} %get-tuple-element.188, s32[64]{0:T(128)S(1)} %compare_select_fusion.4, f32[64,128,256]{2,1,0:T(8,128)} %fusion.38), kind=kCustom, calls=%fused_computation.1.clone.1 | custom fusion | flops 2097152 | bytes 25166080 | tf_op jit(solution)/shard_map/while/body/eval_jaxpr/scatter-add | solution.py:28
  100.9 0.1 compare_and_fusion.2
  101.0 2.8 gather_fusion
  103.7 7.4 %fusion.38 = f32[64,128,256]{2,1,0:T(8,128)} fusion(bf16[64,128,256]{2,1,0:T(8,128)(2,1)} %gather_fusion, pred[64]{0:T(512)(128)(4,1)S(1)} %get-tuple-element.176, bf16[256,128,128]{2,1,0:T(8,128)(2,1)} %get-tuple-element.200, s32[]{:T(128)S(6)} %select_n.59), kind=kOutput, calls=%fused_computation.2.clone.1 | convolution fusion | flops 538968064 | bytes 14680132 | tf_op jit(solution)/shard_map/while/body/eval_jaxpr/gab,gbs->gas/dot_general | solution.py:27
  111.1 0.1 compare_select_fusion.4
  111.2 19.6 %scatter_fusion = f32[32,128,256]{2,1,0:T(8,128)} fusion(f32[32,128,256]{2,1,0:T(8,128)} %get-tuple-element.188, s32[64]{0:T(128)S(1)} %compare_select_fusion.4, f32[64,128,256]{2,1,0:T(8,128)} %fusion.38), kind=kCustom, calls=%fused_computation.1.clone.1 | custom fusion | flops 2097152 | bytes 25166080 | tf_op jit(solution)/shard_map/while/body/eval_jaxpr/scatter-add | solution.py:28
  130.8 0.1 compare_and_fusion.2
  130.9 2.8 gather_fusion
  133.6 7.4 %fusion.38 = f32[64,128,256]{2,1,0:T(8,128)} fusion(bf16[64,128,256]{2,1,0:T(8,128)(2,1)} %gather_fusion, pred[64]{0:T(512)(128)(4,1)S(1)} %get-tuple-element.176, bf16[256,128,128]{2,1,0:T(8,128)(2,1)} %get-tuple-element.200, s32[]{:T(128)S(6)} %select_n.59), kind=kOutput, calls=%fused_computation.2.clone.1 | convolution fusion | flops 538968064 | bytes 14680132 | tf_op jit(solution)/shard_map/while/body/eval_jaxpr/gab,gbs->gas/dot_general | solution.py:27
  141.0 0.1 compare_select_fusion.4
  141.1 19.2 %scatter_fusion = f32[32,128,256]{2,1,0:T(8,128)} fusion(f32[32,128,256]{2,1,0:T(8,128)} %get-tuple-element.188, s32[64]{0:T(128)S(1)} %compare_select_fusion.4, f32[64,128,256]{2,1,0:T(8,128)} %fusion.38), kind=kCustom, calls=%fused_computation.1.clone.1 | custom fusion | flops 2097152 | bytes 25166080 | tf_op jit(solution)/shard_map/while/body/eval_jaxpr/scatter-add | solution.py:28
  160.3 0.0 reduce-scatter.2.cloned.1.call-update
  160.3 0.0 all-reduce.5.cloned.1.call-start
  160.3 50.9 %reduce-scatter.2.cloned.1.call-done = f32[512,256]{1,0:T(8,128)} async-done(((f32[4096,256]{1,0:T(8,128)}), f32[512,256]{1,0:T(8,128)}) %reduce-scatter.2.cloned.1.call-update) | async-done | bytes 524304 | tf_op jit(solution)/shard_map/reduce_scatter | solution.py:48
  211.2 2.2 fusion.11
  213.5 0.0 all-reduce.5.cloned.1.call-update
  213.5 0.0 all-reduce.7.cloned.1.call-start
  213.6 124.1 %all-reduce.5.cloned.1.call-done = f32[128,128]{0,1:T(8,128)} async-done(((f32[128,128]{0,1:T(8,128)}), f32[128,128]{0,1:T(8,128)}) %all-reduce.5.cloned.1.call-update) | async-done | bytes 65552 | tf_op jit(solution)/shard_map/psum | solution.py:53
  337.7 0.8 broadcast_multiply_fusion.2
  338.5 0.1 copy.7
  338.6 0.9 fusion.20
  339.5 11.7 %cholesky.44 = f32[128,128]{1,0:T(8,128)S(1)} custom-call(f32[128,128]{1,0:T(8,128)S(1)} %fusion.20), custom_call_target="Cholesky" | custom-call | tf_op jit(solution)/shard_map/jit(cholesky)/cholesky | solution.py:11
  351.2 0.6 compare_reduce_fusion.1
  351.8 0.7 fusion.22
  352.5 9.8 %custom-call.6 = f32[1,128,128]{1,2,0:T(8,128)S(1)} custom-call(f32[1,128,128]{2,1,0:T(8,128)S(1)} %get-tuple-element.131), custom_call_target="InvertDiagBlocksLowerTriangular" | custom-call | tf_op jit(solution)/shard_map/triangular_solve/custom-call.0 | solution.py:13
  362.3 0.3 fusion.15
  362.6 1.3 fusion.9
  364.0 2.2 fusion.7
  366.1 0.0 all-reduce.7.cloned.1.call-update
  366.2 0.2 all-reduce.9.cloned.1.call-start
  366.4 118.3 %all-reduce.7.cloned.1.call-done = f32[128,128]{0,1:T(8,128)} async-done(((f32[128,128]{0,1:T(8,128)}), f32[128,128]{0,1:T(8,128)}) %all-reduce.7.cloned.1.call-update) | async-done | bytes 65552 | tf_op jit(solution)/shard_map/psum | solution.py:58
  484.7 1.6 convolution_subtract_fusion
  486.3 1.2 fusion.24
  487.5 0.0 all-reduce.9.cloned.1.call-update
  487.5 0.8 broadcast_multiply_fusion.1
  488.3 121.6 %all-reduce.9.cloned.1.call-done = f32[128,128]{0,1:T(8,128)} async-done(((f32[128,128]{0,1:T(8,128)}), f32[128,128]{0,1:T(8,128)}) %all-reduce.9.cloned.1.call-update) | async-done | bytes 65552 | tf_op jit(solution)/shard_map/psum | solution.py:62
  610.0 0.8 broadcast_multiply_fusion
  610.8 0.1 copy.10
  610.9 0.9 fusion.18
  611.8 11.7 %cholesky.55 = f32[128,128]{1,0:T(8,128)S(1)} custom-call(f32[128,128]{1,0:T(8,128)S(1)} %fusion.18), custom_call_target="Cholesky" | custom-call | tf_op jit(solution)/shard_map/jit(cholesky)/cholesky | solution.py:11
  623.5 0.6 compare_reduce_fusion
  624.2 0.7 fusion.23
  624.8 0.8 copy.12
  625.7 9.8 %custom-call.7 = f32[1,128,128]{1,2,0:T(8,128)S(1)} custom-call(f32[1,128,128]{2,1,0:T(8,128)S(1)} %get-tuple-element.133), custom_call_target="InvertDiagBlocksLowerTriangular" | custom-call | tf_op jit(solution)/shard_map/triangular_solve/custom-call.0 | solution.py:13
  635.5 0.3 fusion.13
  635.8 0.4 fusion.25
  636.2 1.0 copy.11
  (9 shorter events, 0.2 us)
Async XLA Ops:
  7.2 32.3 %all-gather.2.cloned.1.call-start = ((), (), s32[]{:S(2)}) async-start(), calls=%async_computation.1 | async-start | bytes 1310720 | tf_op jit(solution)/shard_map/all_gather | solution.py:45
  7.9 203.3 %reduce-scatter.2.cloned.1.call-start = ((), (), s32[]{:S(2)}) async-start(), calls=%async_computation.2 | async-start | bytes 4718592 | tf_op jit(solution)/shard_map/reduce_scatter | solution.py:48
  39.5 2.5 copy-start
  160.3 177.4 %all-reduce.5.cloned.1.call-start = ((), (), s32[]{:S(2)}) async-start(), calls=%async_computation.3 | async-start | bytes 131072 | tf_op jit(solution)/shard_map/psum | solution.py:53
  213.5 271.2 %all-reduce.7.cloned.1.call-start = ((), (), s32[]{:S(2)}) async-start(), calls=%async_computation.4 | async-start | bytes 131072 | tf_op jit(solution)/shard_map/psum | solution.py:58
  366.2 243.8 %all-reduce.9.cloned.1.call-start = ((), (), s32[]{:S(2)}) async-start(), calls=%async_computation.5 | async-start | bytes 131072 | tf_op jit(solution)/shard_map/psum | solution.py:62
Sparse Core Ops, SparseCore 0:
  9.6 29.8 all-gather.1
  160.4 50.7 reduce-scatter.1
  218.3 119.2 all-reduce.4
  366.3 118.3 all-reduce.6
  491.6 118.3 all-reduce.8
where the time goes:
time: 644 us
  waiting for transfers between devices  446 us (69%)
  other arithmetic  128 us (20%)
  matrix products  39 us (6%)
  local copies, waits for them, and re-layouts  15.6 us (2%)
  between operations  13.9 us (2%)
    psum x1, waiting for transfers between devices, on_device(): lax.psum(jnp.dot(first_part.T, first_part, precision=high), ('row', 'col'))  124 us
    psum x1, waiting for transfers between devices, on_device(): lax.psum(jnp.dot(remainder.T, remainder, precision=high), ('row', 'col'))  122 us
    psum x1, waiting for transfers between devices, on_device(): lax.psum(jnp.dot(basis_one.T, second_part, precision=high), ('row', 'col'))  118 us
    scatter-add x4, other arithmetic, advance(): return summed.at[row_ids].add(product)  77.1 us
    reduce_scatter x1, waiting for transfers between devices, on_device(): lax.psum_scatter(partial_value, 'col', scatter_dimension=0, tiled=True)  50.9 us
    all_gather x1, waiting for transfers between devices, on_device(): gathered = lax.all_gather(gaussian_sketch, 'row', axis=0, tiled=True)  30.8 us
    dot_general x4, matrix products, advance(): jnp.einsum('gab,gbs->gas', values, picked, preferred_element_type=jnp.flo...  29.5 us
    another operation x6, other arithmetic, upper_parts(): lower_factor = jnp.linalg.cholesky(gram)  24.8 us
  transfers between devices with their start and end apart: 5, of which 5 were waited for; matrix products, arithmetic and copies ran while one was open for 0% of the time, Pallas kernels for 0%

commit v1 on v0

--- a/solution.py
+++ b/solution.py
@@ -1,3 +1,4 @@
+import functools
 import math
 import jax
 import jax.numpy as jnp
@@ -5,6 +6,15 @@
 from jax.sharding import PartitionSpec as P
 
 PANEL = 128
+
+
+def serve_terms(vals, ax_name, group_axis):
+    for ii in (ax_name, group_axis):
+        vals = jax.lax.psum(vals, axis_name=ii)
+    return vals
+
+
+counts_wrap = functools.partial(serve_terms, ax_name="col", group_axis="row")
 
 
 def upper_parts(gram):
@@ -49,9 +59,7 @@
     first_part = sketched[:, :PANEL]
     second_part = sketched[:, PANEL:]
     order_total = shard_rows * size_row * size_col
-    gram_one = (
-        lax.psum(jnp.dot(first_part.T, first_part, precision=high), ("row", "col")) / order_total
-    )
+    gram_one = counts_wrap(jnp.dot(first_part.T, first_part, precision=high)) / order_total
     upper_one, inverse_one = upper_parts(gram_one)
     basis_one = jnp.dot(first_part, inverse_one, precision=high)
     coupling = (

time: 644 us -> 611 us (0.949)
  waiting for transfers between devices: 446 us -> 413 us
    psum x1 -> x2, waiting for transfers between devices: 124 us -> 87.6 us  [serve_terms(): vals = jax.lax.psum(vals, axis_name=ii)]
  transfers between devices with their start and end apart: 5 -> 6, of which waited for: 5 -> 6; matrix products, arithmetic and copies ran while one was open for 0% -> 0% of each run, Pallas kernels for 0% -> 0%
where the time goes in v1:
time: 611 us; the launch traced here: 610 us
  waiting for transfers between devices  413 us (68%)
  other arithmetic  128 us (21%)
  matrix products  39 us (6%)
  local copies, waits for them, and re-layouts  15.6 us (3%)
  between operations  14.2 us (2%)
    psum x1, waiting for transfers between devices, on_device(): lax.psum(jnp.dot(remainder.T, remainder, precision=high), ('row', 'col'))  122 us
    psum x1, waiting for transfers between devices, on_device(): lax.psum(jnp.dot(basis_one.T, second_part, precision=high), ('row', 'col'))  121 us
    psum x2, waiting for transfers between devices, serve_terms(): vals = jax.lax.psum(vals, axis_name=ii)  87.6 us
    scatter-add x4, other arithmetic, advance(): return summed.at[row_ids].add(product)  77.1 us
    reduce_scatter x1, waiting for transfers between devices, on_device(): lax.psum_scatter(partial_value, 'col', scatter_dimension=0, tiled=True)  50.9 us
    all_gather x1, waiting for transfers between devices, on_device(): gathered = lax.all_gather(gaussian_sketch, 'row', axis=0, tiled=True)  30.8 us
    dot_general x4, matrix products, advance(): jnp.einsum('gab,gbs->gas', values, picked, preferred_element_type=jnp.flo...  29.5 us
    another operation x6, other arithmetic, upper_parts(): lower_factor = jnp.linalg.cholesky(gram)  24.8 us
  transfers between devices with their start and end apart: 6, of which 6 were waited for; matrix products, arithmetic and copies ran while one was open for 0% of the time, Pallas kernels for 0%

profile of v1, /device:TPU:1, one launch (start us, length us, event | category | flops | bytes accessed | tf_op | source)
XLA Modules:
  0.0 610.3 jit_solution(32088975091075820)
XLA Ops:
  7.2 0.0 all-gather.2.cloned.1.call-start
  7.2 0.7 all-gather.2.cloned.1.call-update
  7.9 0.0 reduce-scatter.2.cloned.1.call-start
  8.0 0.7 broadcast_subtract_fusion
  8.7 30.8 %all-gather.2.cloned.1.call-done = bf16[2048,256]{1,0:T(8,128)(2,1)} async-done(((bf16[512,256]{1,0:T(8,128)(2,1)}), bf16[2048,256]{1,0:T(8,128)(2,1)}) %all-gather.2.cloned.1.call-update) | async-done | bytes 1048592 | tf_op jit(solution)/shard_map/all_gather | solution.py:55
  39.5 2.5 broadcast_in_dim.36
  41.9 118.3 %while.13 = (s32[]{:T(128)}, f32[32,128,256]{2,1,0:T(8,128)}, s32[256]{0:T(256)S(1)}, bf16[256,128,128]{2,1,0:T(8,128)(2,1)}, s32[256]{0:T(256)S(1)}, /*index=5*...) while((s32[]{:T(128)}, f32[32,128,256]{2,1,0:T(8,128)}, s32[256]{0:T(256)S(1)}, ...), condition=%wide.region_2.3_spmd, body=%wide.region_0.2_spmd.sunk | while | flops 541066816 | bytes 48240672 | solution.py:41
  41.9 0.1 compare_and_fusion.2
  42.0 2.8 gather_fusion
  44.8 7.4 %fusion.38 = f32[64,128,256]{2,1,0:T(8,128)} fusion(bf16[64,128,256]{2,1,0:T(8,128)(2,1)} %gather_fusion, pred[64]{0:T(512)(128)(4,1)S(1)} %get-tuple-element.176, bf16[256,128,128]{2,1,0:T(8,128)(2,1)} %get-tuple-element.200, s32[]{:T(128)S(6)} %select_n.59), kind=kOutput, calls=%fused_computation.2.clone.1 | convolution fusion | flops 538968064 | bytes 14680132 | tf_op jit(solution)/shard_map/while/body/eval_jaxpr/gab,gbs->gas/dot_general | solution.py:37
  52.2 0.1 compare_select_fusion.4
  52.3 19.2 %scatter_fusion = f32[32,128,256]{2,1,0:T(8,128)} fusion(f32[32,128,256]{2,1,0:T(8,128)} %get-tuple-element.188, s32[64]{0:T(128)S(1)} %compare_select_fusion.4, f32[64,128,256]{2,1,0:T(8,128)} %fusion.38), kind=kCustom, calls=%fused_computation.1.clone.1 | custom fusion | flops 2097152 | bytes 25166080 | tf_op jit(solution)/shard_map/while/body/eval_jaxpr/scatter-add | solution.py:38
  71.4 0.1 compare_and_fusion.2
  71.5 2.8 gather_fusion
  74.3 7.4 %fusion.38 = f32[64,128,256]{2,1,0:T(8,128)} fusion(bf16[64,128,256]{2,1,0:T(8,128)(2,1)} %gather_fusion, pred[64]{0:T(512)(128)(4,1)S(1)} %get-tuple-element.176, bf16[256,128,128]{2,1,0:T(8,128)(2,1)} %get-tuple-element.200, s32[]{:T(128)S(6)} %select_n.59), kind=kOutput, calls=%fused_computation.2.clone.1 | convolution fusion | flops 538968064 | bytes 14680132 | tf_op jit(solution)/shard_map/while/body/eval_jaxpr/gab,gbs->gas/dot_general | solution.py:37
  81.7 0.1 compare_select_fusion.4
  81.7 19.1 %scatter_fusion = f32[32,128,256]{2,1,0:T(8,128)} fusion(f32[32,128,256]{2,1,0:T(8,128)} %get-tuple-element.188, s32[64]{0:T(128)S(1)} %compare_select_fusion.4, f32[64,128,256]{2,1,0:T(8,128)} %fusion.38), kind=kCustom, calls=%fused_computation.1.clone.1 | custom fusion | flops 2097152 | bytes 25166080 | tf_op jit(solution)/shard_map/while/body/eval_jaxpr/scatter-add | solution.py:38
  100.9 0.1 compare_and_fusion.2
  101.0 2.8 gather_fusion
  103.7 7.4 %fusion.38 = f32[64,128,256]{2,1,0:T(8,128)} fusion(bf16[64,128,256]{2,1,0:T(8,128)(2,1)} %gather_fusion, pred[64]{0:T(512)(128)(4,1)S(1)} %get-tuple-element.176, bf16[256,128,128]{2,1,0:T(8,128)(2,1)} %get-tuple-element.200, s32[]{:T(128)S(6)} %select_n.59), kind=kOutput, calls=%fused_computation.2.clone.1 | convolution fusion | flops 538968064 | bytes 14680132 | tf_op jit(solution)/shard_map/while/body/eval_jaxpr/gab,gbs->gas/dot_general | solution.py:37
  111.1 0.1 compare_select_fusion.4
  111.2 19.6 %scatter_fusion = f32[32,128,256]{2,1,0:T(8,128)} fusion(f32[32,128,256]{2,1,0:T(8,128)} %get-tuple-element.188, s32[64]{0:T(128)S(1)} %compare_select_fusion.4, f32[64,128,256]{2,1,0:T(8,128)} %fusion.38), kind=kCustom, calls=%fused_computation.1.clone.1 | custom fusion | flops 2097152 | bytes 25166080 | tf_op jit(solution)/shard_map/while/body/eval_jaxpr/scatter-add | solution.py:38
  130.8 0.1 compare_and_fusion.2
  130.9 2.8 gather_fusion
  133.6 7.4 %fusion.38 = f32[64,128,256]{2,1,0:T(8,128)} fusion(bf16[64,128,256]{2,1,0:T(8,128)(2,1)} %gather_fusion, pred[64]{0:T(512)(128)(4,1)S(1)} %get-tuple-element.176, bf16[256,128,128]{2,1,0:T(8,128)(2,1)} %get-tuple-element.200, s32[]{:T(128)S(6)} %select_n.59), kind=kOutput, calls=%fused_computation.2.clone.1 | convolution fusion | flops 538968064 | bytes 14680132 | tf_op jit(solution)/shard_map/while/body/eval_jaxpr/gab,gbs->gas/dot_general | solution.py:37
  141.0 0.1 compare_select_fusion.4
  141.1 19.2 %scatter_fusion = f32[32,128,256]{2,1,0:T(8,128)} fusion(f32[32,128,256]{2,1,0:T(8,128)} %get-tuple-element.188, s32[64]{0:T(128)S(1)} %compare_select_fusion.4, f32[64,128,256]{2,1,0:T(8,128)} %fusion.38), kind=kCustom, calls=%fused_computation.1.clone.1 | custom fusion | flops 2097152 | bytes 25166080 | tf_op jit(solution)/shard_map/while/body/eval_jaxpr/scatter-add | solution.py:38
  160.3 0.0 reduce-scatter.2.cloned.1.call-update
  160.3 0.0 all-reduce.6.cloned.1.call-start
  160.3 50.9 %reduce-scatter.2.cloned.1.call-done = f32[512,256]{1,0:T(8,128)} async-done(((f32[4096,256]{1,0:T(8,128)}), f32[512,256]{1,0:T(8,128)}) %reduce-scatter.2.cloned.1.call-update) | async-done | bytes 524304 | tf_op jit(solution)/shard_map/reduce_scatter | solution.py:58
  211.2 2.2 fusion.11
  213.5 0.0 all-reduce.6.cloned.1.call-update
  213.5 0.0 all-reduce.8.cloned.1.call-start
  213.6 53.4 %all-reduce.6.cloned.1.call-done = f32[128,128]{0,1:T(8,128)} async-done(((f32[128,128]{0,1:T(8,128)}), f32[128,128]{0,1:T(8,128)}) %all-reduce.6.cloned.1.call-update) | async-done | bytes 65552 | tf_op jit(solution)/shard_map/psum | solution.py:13
  267.0 0.0 all-reduce.8.cloned.1.call-update
  267.0 0.0 all-reduce.10.cloned.1.call-start
  267.0 34.2 %all-reduce.8.cloned.1.call-done = f32[128,128]{0,1:T(8,128)} async-done(((f32[128,128]{0,1:T(8,128)}), f32[128,128]{0,1:T(8,128)}) %all-reduce.8.cloned.1.call-update) | async-done | bytes 65552 | tf_op jit(solution)/shard_map/psum | solution.py:13
  301.3 0.8 broadcast_multiply_fusion.2
  302.1 0.1 copy.7
  302.2 0.9 fusion.20
  303.1 11.7 %cholesky.44 = f32[128,128]{1,0:T(8,128)S(1)} custom-call(f32[128,128]{1,0:T(8,128)S(1)} %fusion.20), custom_call_target="Cholesky" | custom-call | tf_op jit(solution)/shard_map/jit(cholesky)/cholesky | solution.py:21
  314.8 0.6 compare_reduce_fusion.1
  315.5 0.7 fusion.22
  316.1 9.8 %custom-call.6 = f32[1,128,128]{1,2,0:T(8,128)S(1)} custom-call(f32[1,128,128]{2,1,0:T(8,128)S(1)} %get-tuple-element.131), custom_call_target="InvertDiagBlocksLowerTriangular" | custom-call | tf_op jit(solution)/shard_map/triangular_solve/custom-call.0 | solution.py:23
  325.9 0.3 fusion.15
  326.2 1.3 fusion.9
  327.6 2.2 fusion.7
  329.8 0.2 all-reduce.12.cloned.1.call-start
  330.0 120.9 %all-reduce.10.cloned.1.call-done = f32[128,128]{0,1:T(8,128)} async-done(((f32[128,128]{0,1:T(8,128)}), f32[128,128]{0,1:T(8,128)}) %all-reduce.10.cloned.1.call-update) | async-done | bytes 65552 | tf_op jit(solution)/shard_map/psum | solution.py:66
  450.9 1.6 convolution_subtract_fusion
  452.5 1.2 fusion.24
  453.7 0.8 broadcast_multiply_fusion.1
  454.6 121.6 %all-reduce.12.cloned.1.call-done = f32[128,128]{0,1:T(8,128)} async-done(((f32[128,128]{0,1:T(8,128)}), f32[128,128]{0,1:T(8,128)}) %all-reduce.12.cloned.1.call-update) | async-done | bytes 65552 | tf_op jit(solution)/shard_map/psum | solution.py:70
  576.2 0.8 broadcast_multiply_fusion
  577.0 0.1 copy.10
  577.1 0.9 fusion.18
  578.0 11.7 %cholesky.55 = f32[128,128]{1,0:T(8,128)S(1)} custom-call(f32[128,128]{1,0:T(8,128)S(1)} %fusion.18), custom_call_target="Cholesky" | custom-call | tf_op jit(solution)/shard_map/jit(cholesky)/cholesky | solution.py:21
  589.7 0.6 compare_reduce_fusion
  590.4 0.7 fusion.23
  591.1 0.8 copy.12
  591.9 9.8 %custom-call.7 = f32[1,128,128]{1,2,0:T(8,128)S(1)} custom-call(f32[1,128,128]{2,1,0:T(8,128)S(1)} %get-tuple-element.133), custom_call_target="InvertDiagBlocksLowerTriangular" | custom-call | tf_op jit(solution)/shard_map/triangular_solve/custom-call.0 | solution.py:23
  601.7 0.3 fusion.13
  602.0 0.4 fusion.25
  602.5 1.0 copy.11
  (12 shorter events, 0.2 us)
Async XLA Ops:
  7.2 32.3 %all-gather.2.cloned.1.call-start = ((), (), s32[]{:S(2)}) async-start(), calls=%async_computation.1 | async-start | bytes 1310720 | tf_op jit(solution)/shard_map/all_gather | solution.py:55
  7.9 203.3 %reduce-scatter.2.cloned.1.call-start = ((), (), s32[]{:S(2)}) async-start(), calls=%async_computation.2 | async-start | bytes 4718592 | tf_op jit(solution)/shard_map/reduce_scatter | solution.py:58
  39.5 2.5 copy-start
  160.3 106.7 %all-reduce.6.cloned.1.call-start = ((), (), s32[]{:S(2)}) async-start(), calls=%async_computation.3 | async-start | bytes 131072 | tf_op jit(solution)/shard_map/psum | solution.py:13
  213.5 87.8 %all-reduce.8.cloned.1.call-start = ((), (), s32[]{:S(2)}) async-start(), calls=%async_computation.4 | async-start | bytes 131072 | tf_op jit(solution)/shard_map/psum | solution.py:13
  267.0 183.9 %all-reduce.10.cloned.1.call-start = ((), (), s32[]{:S(2)}) async-start(), calls=%async_computation.5 | async-start | bytes 131072 | tf_op jit(solution)/shard_map/psum | solution.py:66
  329.8 246.4 %all-reduce.12.cloned.1.call-start = ((), (), s32[]{:S(2)}) async-start(), calls=%async_computation.6 | async-start | bytes 131072 | tf_op jit(solution)/shard_map/psum | solution.py:70
Sparse Core Ops, SparseCore 0:
  9.6 29.8 all-gather.1
  160.4 50.7 reduce-scatter.1
  215.2 51.7 all-reduce.5
  269.1 32.0 all-reduce.7
  329.9 120.9 all-reduce.9
  457.8 118.3 all-reduce.11
